TPU v7x, 32 devices: a whole 2x2x4 slice. The times are simulated.
32 devices in a mesh: samp: 8 (over y, x, core), sx: 2 (over z_hi), sy: 2 (over z_lo).
Axes of the slice: x: 2, y: 2, z: 4 (z_hi: 2, z_lo: 2; z = z_hi * 2 + z_lo), core: 2. Of those that a mesh axis runs over, the one named last changes fastest.
Arguments:
- volume: bfloat16 [8, 32, 4, 16, 128], P('samp', None, 'sx', 'sy'), may hold values from -6 to 6
- kernel: bfloat16 [64, 32, 3, 3, 3], replicated, may hold values from -0.21875 to 0.21875
- bias: float32 [64], replicated, may hold values from -4 to 4
- upstream: bfloat16 [8, 64, 4, 16, 128], P('samp', None, 'sx', 'sy'), may hold values from -6 to 6
Outputs:
- activated: bfloat16 [8, 64, 4, 16, 128], P('samp', None, 'sx', 'sy')
- input_grad: bfloat16 [8, 32, 4, 16, 128], P('samp', None, 'sx', 'sy')
- filter_grad: float32 [64, 32, 3, 3, 3], replicated
- bias_grad: float32 [64], replicated
All inputs are finite; a program needn't handle non-finite values.
Results may differ from a plain program's by a relative error of at most 0.0065.
Values may be sent and summed in bfloat16 or wider, within the bound.
A program may use at most 64 MiB of HBM per device.

v0:
```python
import jax
import jax.numpy as jnp
from jax import lax
from jax.sharding import PartitionSpec as P


def extended(shard, sides, width):
    for axis, dim in sides:
        size, length = (lax.axis_size(axis), shard.shape[dim])
        up = [(i, (i + 1) % size) for i in range(size - 1)]
        down = [(j, i) for i, j in up]
        last = lax.slice_in_dim(shard, length - width, length, axis=dim)
        initial = lax.slice_in_dim(shard, 0, width, axis=dim)
        before = lax.ppermute(last, axis, up)
        after = lax.ppermute(initial, axis, down)
        shard = jnp.concatenate([before, shard, after], axis=dim)
    return shard


def conv_forward(padded, kernel):
    return lax.conv_general_dilated(
        padded,
        kernel,
        (1, 1, 1),
        ((0, 0), (0, 0), (1, 1)),
        dimension_numbers=("NCDHW", "OIDHW", "NCDHW"),
        preferred_element_type=jnp.float32,
    )


def conv_backward(padded, kernel):
    flipped = kernel[:, :, ::-1, ::-1, ::-1]
    return lax.conv_general_dilated(
        padded,
        flipped,
        (1, 1, 1),
        ((0, 0), (0, 0), (1, 1)),
        dimension_numbers=("NCDHW", "IODHW", "NCDHW"),
        preferred_element_type=jnp.float32,
    )


def filter_terms(padded, delta):
    return lax.conv_general_dilated(
        padded,
        delta,
        (1, 1, 1),
        ((0, 0), (0, 0), (1, 1)),
        dimension_numbers=("CNDHW", "IODHW", "CNDHW"),
        preferred_element_type=jnp.float32,
    )


def slope_of(pre):
    return 0.3 + 0.7 * jax.nn.sigmoid(pre)


def per_device(volume, kernel, bias, upstream):
    samples, rows, cols, depth = (
        volume.shape[0],
        volume.shape[2],
        volume.shape[3],
        volume.shape[4],
    )
    bias_wide = bias[None, :, None, None, None]
    padded = extended(volume, (("sx", 2), ("sy", 3)), 1)
    pre = conv_forward(padded, kernel) + bias_wide
    delta = (upstream.astype(jnp.float32) * slope_of(pre)).astype(jnp.bfloat16)
    delta_pad = extended(delta, (("sx", 2), ("sy", 3)), 1)
    activated = (0.3 * pre + 0.7 * jax.nn.softplus(pre)).astype(jnp.bfloat16)
    input_grad = conv_backward(delta_pad, kernel).astype(jnp.bfloat16)
    wgrad = filter_terms(padded, delta)
    bgrad = jnp.sum(delta.astype(jnp.float32), axis=(0, 2, 3, 4))
    groups = lax.axis_size("sx") * lax.axis_size("sy")
    whole = lax.axis_size("samp") * samples * groups * rows * cols * depth
    norm = 1.0 / jnp.sqrt(jnp.float32(whole))
    wsum, bsum = lax.psum((wgrad, bgrad), ("samp", "sx", "sy"))
    return (activated, input_grad, wsum * norm, bsum * norm)


def solution(mesh):
    in_specs = (P("samp", None, "sx", "sy", None), P(), P(), P("samp", None, "sx", "sy", None))
    out_specs = (P("samp", None, "sx", "sy", None), P("samp", None, "sx", "sy", None), P(), P())
    return jax.shard_map(
        per_device, mesh=mesh, in_specs=in_specs, out_specs=out_specs, check_vma=False
    )
```

profile of v0, /device:TPU:0, one launch (start us, length us, event | category | flops | bytes accessed | tf_op | source)
XLA Modules:
  0.0 222.2 jit_solution(1578653945424406039)
XLA Ops:
  7.2 0.0 copy-start
  7.2 0.0 all-reduce.2.cloned.1.call-start
  7.2 0.9 fusion.47
  8.2 1.3 collective-permute-start.1
  9.5 6.0 %collective-permute-start = (bf16[1,32,1,8,128]{4,3,2,1,0:T(8,128)(2,1)S(1)}, bf16[1,32,1,8,128]{4,3,2,1,0:T(8,128)(2,1)S(1)}, u32[]{:S(2)}, u32[]{:S(2)}) collective-permute-start(bf16[1,32,1,8,128]{4,3,2,1,0:T(8,128)(2,1)S(1)} %get-tuple-element.26), channel_id=1, source_target_pairs={{0,2},{1,3},{4,6},{5,7},{8,10},{9,11},{12,14},{13,15},{16,18},{17,... | collective-permute-start | bytes 196616 | tf_op jit(solution)/shard_map/ppermute | solution.py:14
  15.4 0.3 collective-permute-done.1
  15.7 1.6 collective-permute-done
  17.3 1.0 pad_maximum_fusion.2
  18.3 0.0 copy-start.3
  18.3 1.2 copy.49
  19.5 1.3 fusion.44
  20.8 1.3 collective-permute-start.3
  22.1 5.3 %collective-permute-start.2 = (bf16[1,32,4,1,128]{1,0,4,3,2:T(2,128)(2,1)}, bf16[1,32,4,1,128]{1,0,4,3,2:T(2,128)(2,1)}, u32[]{:S(2)}, u32[]{:S(2)}) collective-permute-start(bf16[1,32,4,1,128]{1,0,4,3,2:T(2,128)(2,1)} %get-tuple-element.18), channel_id=1, source_target_pairs={{0,1},{2,3},{4,5},{6,7},{8,9},{10,11},{12,13},{14,15},{16,17},{18,... | collective-permute-start | bytes 98312 | tf_op jit(solution)/shard_map/ppermute | solution.py:14
  27.4 0.0 copy-done.3
  27.4 0.4 copy.57
  27.8 2.8 %collective-permute-done.3 = bf16[1,32,4,1,128]{1,0,4,3,2:T(2,128)(2,1)S(1)} collective-permute-done((bf16[1,32,4,1,128]{1,0,4,3,2:T(2,128)(2,1)}, bf16[1,32,4,1,128]{1,0,4,3,2:T(2,128)(2,1)S(1)}, u32[]{:S(2)}, u32[]{:S(2)}) %collective-permute-start.3) | collective-permute-done | bytes 32800 | tf_op jit(solution)/shard_map/ppermute | solution.py:15
  30.6 1.3 collective-permute-done.2
  31.9 6.7 %pad_maximum_fusion = bf16[1,32,4,10,128]{1,0,4,3,2:T(2,128)(2,1)} fusion(bf16[1,32,4,1,128]{1,0,4,3,2:T(2,128)(2,1)S(1)} %collective-permute-done.3, bf16[1,32,4,8,128]{1,0,4,3,2:T(2,128)(2,1)S(1)} %copy.49, bf16[1,32,4,1,128]{1,0,4,3,2:T(2,128)(2,1)} %collective-permute-done.2), kind=kLoop, calls=%fused_computation.5 | loop fusion | flops 327680 | bytes 655360 | tf_op jit(solution)/shard_map/concatenate | solution.py:16
  38.6 4.7 %copy.52 = bf16[1,32,4,10,128]{4,1,3,2,0:T(8,128)(2,1)S(1)} copy(bf16[1,32,4,10,128]{1,0,4,3,2:T(2,128)(2,1)} %pad_maximum_fusion) | data formatting | bytes 655360 | tf_op jit(solution)/shard_map/concatenate | solution.py:16
  43.3 1.0 copy.69
  44.3 0.7 pad.clone
  45.0 0.0 copy-start.7
  45.0 0.0 copy-start.8
  45.0 0.2 copy.55
  45.3 0.4 copy-done.7
  45.7 0.0 copy-done.8
  45.7 3.4 %multiply_add_fusion = (f32[2,8,8,17,64]{4,2,3,1,0:T(8,128)S(1)}, bf16[2,8,8,17,64]{4,2,3,1,0:T(8,128)(2,1)}) fusion(f32[64]{0:T(128)S(1)} %copy-done.7, bf16[64,32,3,3,3]{0,1,4,3,2:T(8,128)(2,1)S(1)} %copy-done, bf16[32,4,10,1,7,2]{0,4,5,2,1,3:T(8,128)(2,1)S(1)} %slice.39, bf16[32,4,10,1,8,17]{0,4,5,2,1,3:T(8,128)(2,1)S(1)} %copy.55, ...), kind=kOutput, calls=%fused_computation.25 | convolution fusion | flops 244183040 | bytes 1330568 | tf_op jit(solution)/shard_map/conv_general_dilated | solution.py:21
  49.1 0.2 copy.58
  49.4 0.8 convert_reduce_fusion
  50.2 0.8 fusion.46
  51.0 0.1 copy-done.1
  51.1 15.8 %fusion.33 = f32[64,32,3,3,3]{0,1,4,3,2:T(8,128)} fusion(bf16[1,32,4,10,128]{1,0,4,3,2:T(2,128)(2,1)S(1)} %copy-done.1, bf16[1,64,2,8,128]{1,3,4,2,0:T(8,128)(2,1)S(1)} %get-tuple-element.17), kind=kOutput, calls=%fused_computation.31 | convolution fusion | flops 225312768 | bytes 811008 | tf_op jit(solution)/shard_map/conv_general_dilated | solution.py:44
  66.9 0.0 copy-done.2
  66.9 0.1 copy.56
  67.0 0.0 copy-start.6
  67.0 1.1 copy.67
  68.2 0.0 copy-done.5
  68.2 1.3 collective-permute-start.5
  69.5 5.5 %collective-permute-start.4 = (bf16[1,64,1,8,128]{1,3,4,2,0:T(8,128)(2,1)S(1)}, bf16[1,64,1,8,128]{1,3,4,2,0:T(8,128)(2,1)S(1)}, u32[]{:S(2)}, u32[]{:S(2)}) collective-permute-start(bf16[1,64,1,8,128]{1,3,4,2,0:T(8,128)(2,1)S(1)} %copy-done.4), channel_id=1, source_target_pairs={{0,2},{1,3},{4,6},{5,7},{8,10},{9,11},{12,14},{13,15},{16,18},{17,... | collective-permute-start | bytes 393224 | tf_op jit(solution)/shard_map/ppermute | solution.py:14
  75.0 0.0 all-reduce.2.cloned.1.call-update
  75.0 41.5 %psum.15 = f32[64]{0:T(128)S(1)} all-reduce(f32[64]{0:T(128)S(1)} %copy-done.6), channel_id=1, replica_groups=mesh['samp'=8,'sx'=2,'sy'=2] {'samp','sx','sy'}, use_global_device_ids=true, to_apply=%region_2.3 | all-reduce | flops 64 | bytes 512 | tf_op jit(solution)/shard_map/psum | solution.py:77
  116.5 0.5 broadcast_multiply_fusion.1
  117.0 0.0 collective-permute-done.5
  117.0 0.0 collective-permute-done.4
  117.0 0.2 pad_maximum_fusion.1
  117.3 0.3 fusion.45
  117.6 1.3 collective-permute-start.7
  118.9 4.6 %collective-permute-start.6 = (bf16[1,64,4,1,128]{1,3,4,2,0:T(2,128)(2,1)S(1)}, bf16[1,64,4,1,128]{1,3,4,2,0:T(2,128)(2,1)S(1)}, u32[]{:S(2)}, u32[]{:S(2)}) collective-permute-start(bf16[1,64,4,1,128]{1,3,4,2,0:T(2,128)(2,1)S(1)} %get-tuple-element.22), channel_id=1, source_target_pairs={{0,1},{2,3},{4,5},{6,7},{8,9},{10,11},{12,13},{14,15},{16,17},{18,... | collective-permute-start | bytes 196616 | tf_op jit(solution)/shard_map/ppermute | solution.py:14
  123.5 80.6 %all-reduce.2.cloned.1.call-done = f32[64,32,3,3,3]{0,1,4,3,2:T(8,128)} async-done(((f32[64,32,3,3,3]{0,1,4,3,2:T(8,128)}), f32[64,32,3,3,3]{0,1,4,3,2:T(8,128)}) %all-reduce.2.cloned.1.call-update) | async-done | bytes 221200 | tf_op jit(solution)/shard_map/psum | solution.py:77
  204.0 1.8 broadcast_multiply_fusion
  205.9 0.6 copy.60
  206.5 0.0 collective-permute-done.7
  206.5 0.1 copy.61
  206.6 0.0 collective-permute-done.6
  206.6 0.1 copy.59
  206.8 0.1 maximum_bitcast_fusion
  206.9 1.9 copy.70
  208.7 0.7 pad.2.clone
  209.4 0.0 copy-start.9
  209.4 0.2 copy.64
  209.7 0.4 copy-done.9
  210.1 4.0 %fusion.25 = bf16[2,8,8,17,32]{4,2,3,1,0:T(8,128)(2,1)S(1)} fusion(bf16[64,32,3,3,3]{0,1,4,3,2:T(8,128)(2,1)S(1)} %copy-done, bf16[64,4,10,1,7,2]{0,4,5,2,1,3:T(8,128)(2,1)S(1)} %slice.46, bf16[64,4,10,1,8,17]{0,4,5,2,1,3:T(8,128)(2,1)S(1)} %copy.64, pred[8,17]{0,1:T(8,128)(4,1)S(1)} %copy-done.9), kind=kOutput, calls=%fused_computation.21 | convolution fusion | flops 243122176 | bytes 1017992 | tf_op jit(solution)/shard_map/conv_general_dilated | solution.py:33
  214.2 0.1 copy.65
  214.3 1.0 copy.68
  (11 shorter events, 0.2 us)
Async XLA Ops:
  7.2 38.1 %copy-start = (bf16[64,32,3,3,3]{0,1,4,3,2:T(8,128)(2,1)S(1)}, bf16[64,32,3,3,3]{0,1,4,3,2:T(8,128)(2,1)}, u32[]{:S(2)}) copy-start(bf16[64,32,3,3,3]{0,1,4,3,2:T(8,128)(2,1)} %param.5) | copy-start | bytes 331780
  7.2 196.9 %all-reduce.2.cloned.1.call-start = ((), (), s32[]{:S(2)}) async-start(), calls=%async_computation | async-start | bytes 884736 | tf_op jit(solution)/shard_map/psum | solution.py:77
  8.2 7.6 %collective-permute-start.1 = (bf16[1,32,1,8,128]{4,3,2,1,0:T(8,128)(2,1)S(1)}, bf16[1,32,1,8,128]{4,3,2,1,0:T(8,128)(2,1)S(1)}, u32[]{:S(2)}, u32[]{:S(2)}) collective-permute-start(bf16[1,32,1,8,128]{4,3,2,1,0:T(8,128)(2,1)S(1)} %get-tuple-element.27), channel_id=1, source_target_pairs={{2,0},{3,1},{6,4},{7,5},{10,8},{11,9},{14,12},{15,13},{18,16},{19,... | collective-permute-start | bytes 196616 | tf_op jit(solution)/shard_map/ppermute | solution.py:15
  9.5 7.9 %collective-permute-start = (bf16[1,32,1,8,128]{4,3,2,1,0:T(8,128)(2,1)S(1)}, bf16[1,32,1,8,128]{4,3,2,1,0:T(8,128)(2,1)S(1)}, u32[]{:S(2)}, u32[]{:S(2)}) collective-permute-start(bf16[1,32,1,8,128]{4,3,2,1,0:T(8,128)(2,1)S(1)} %get-tuple-element.26), channel_id=1, source_target_pairs={{0,2},{1,3},{4,6},{5,7},{8,10},{9,11},{12,14},{13,15},{16,18},{17,... | collective-permute-start | bytes 196616 | tf_op jit(solution)/shard_map/ppermute | solution.py:14
  18.3 9.1 %copy-start.3 = (bf16[1,64,2,8,128]{4,3,2,1,0:T(8,128)(2,1)S(1)}, bf16[1,64,2,8,128]{4,3,2,1,0:T(8,128)(2,1)}, u32[]{:S(2)}) copy-start(bf16[1,64,2,8,128]{4,3,2,1,0:T(8,128)(2,1)} %param.7) | copy-start | bytes 786436
  20.8 9.8 %collective-permute-start.3 = (bf16[1,32,4,1,128]{1,0,4,3,2:T(2,128)(2,1)}, bf16[1,32,4,1,128]{1,0,4,3,2:T(2,128)(2,1)S(1)}, u32[]{:S(2)}, u32[]{:S(2)}) collective-permute-start(bf16[1,32,4,1,128]{1,0,4,3,2:T(2,128)(2,1)} %get-tuple-element.19), channel_id=1, source_target_pairs={{1,0},{3,2},{5,4},{7,6},{9,8},{11,10},{13,12},{15,14},{17,16},{19,... | collective-permute-start | bytes 98312 | tf_op jit(solution)/shard_map/ppermute | solution.py:15
  22.1 9.8 %collective-permute-start.2 = (bf16[1,32,4,1,128]{1,0,4,3,2:T(2,128)(2,1)}, bf16[1,32,4,1,128]{1,0,4,3,2:T(2,128)(2,1)}, u32[]{:S(2)}, u32[]{:S(2)}) collective-permute-start(bf16[1,32,4,1,128]{1,0,4,3,2:T(2,128)(2,1)} %get-tuple-element.18), channel_id=1, source_target_pairs={{0,1},{2,3},{4,5},{6,7},{8,9},{10,11},{12,13},{14,15},{16,17},{18,... | collective-permute-start | bytes 98312 | tf_op jit(solution)/shard_map/ppermute | solution.py:14
  45.0 0.7 copy-start.7
  45.0 0.7 copy-start.8
  49.3 1.7 copy-start.1
  51.1 15.8 %copy-start.2 = (bf16[2,8,8,17,64]{4,2,3,1,0:T(8,128)(2,1)S(1)}, bf16[2,8,8,17,64]{4,2,3,1,0:T(8,128)(2,1)}, u32[]{:S(2)}) copy-start(bf16[2,8,8,17,64]{4,2,3,1,0:T(8,128)(2,1)} %get-tuple-element.21) | copy-start | bytes 835588
  66.9 1.3 copy-start.5
  66.9 2.6 %copy-start.4 = (bf16[1,64,1,8,128]{1,3,4,2,0:T(8,128)(2,1)S(1)}, bf16[1,64,1,8,128]{1,3,4,2,0:T(8,128)(2,1)}, u32[]{:S(2)}) copy-start(bf16[1,64,1,8,128]{1,3,4,2,0:T(8,128)(2,1)} %get-tuple-element.24) | copy-start | bytes 393220
  67.0 8.0 %copy-start.6 = (f32[64]{0:T(128)S(1)}, f32[64]{0:T(128)}, u32[]{:S(2)}) copy-start(f32[64]{0:T(128)} %get-tuple-element.16) | copy-start | bytes 772
  68.2 48.8 %collective-permute-start.5 = (bf16[1,64,1,8,128]{1,3,4,2,0:T(8,128)(2,1)S(1)}, bf16[1,64,1,8,128]{1,3,4,2,0:T(8,128)(2,1)S(1)}, u32[]{:S(2)}, u32[]{:S(2)}) collective-permute-start(bf16[1,64,1,8,128]{1,3,4,2,0:T(8,128)(2,1)S(1)} %copy-done.5), channel_id=1, source_target_pairs={{2,0},{3,1},{6,4},{7,5},{10,8},{11,9},{14,12},{15,13},{18,16},{19,... | collective-permute-start | bytes 393224 | tf_op jit(solution)/shard_map/ppermute | solution.py:15
  69.5 47.5 %collective-permute-start.4 = (bf16[1,64,1,8,128]{1,3,4,2,0:T(8,128)(2,1)S(1)}, bf16[1,64,1,8,128]{1,3,4,2,0:T(8,128)(2,1)S(1)}, u32[]{:S(2)}, u32[]{:S(2)}) collective-permute-start(bf16[1,64,1,8,128]{1,3,4,2,0:T(8,128)(2,1)S(1)} %copy-done.4), channel_id=1, source_target_pairs={{0,2},{1,3},{4,6},{5,7},{8,10},{9,11},{12,14},{13,15},{16,18},{17,... | collective-permute-start | bytes 393224 | tf_op jit(solution)/shard_map/ppermute | solution.py:14
  117.6 88.9 %collective-permute-start.7 = (bf16[1,64,4,1,128]{1,3,4,2,0:T(2,128)(2,1)S(1)}, bf16[1,64,4,1,128]{1,3,4,2,0:T(2,128)(2,1)S(1)}, u32[]{:S(2)}, u32[]{:S(2)}) collective-permute-start(bf16[1,64,4,1,128]{1,3,4,2,0:T(2,128)(2,1)S(1)} %get-tuple-element.23), channel_id=1, source_target_pairs={{1,0},{3,2},{5,4},{7,6},{9,8},{11,10},{13,12},{15,14},{17,16},{19,... | collective-permute-start | bytes 196616 | tf_op jit(solution)/shard_map/ppermute | solution.py:15
  118.9 87.7 %collective-permute-start.6 = (bf16[1,64,4,1,128]{1,3,4,2,0:T(2,128)(2,1)S(1)}, bf16[1,64,4,1,128]{1,3,4,2,0:T(2,128)(2,1)S(1)}, u32[]{:S(2)}, u32[]{:S(2)}) collective-permute-start(bf16[1,64,4,1,128]{1,3,4,2,0:T(2,128)(2,1)S(1)} %get-tuple-element.22), channel_id=1, source_target_pairs={{0,1},{2,3},{4,5},{6,7},{8,9},{10,11},{12,13},{14,15},{16,17},{18,... | collective-permute-start | bytes 196616 | tf_op jit(solution)/shard_map/ppermute | solution.py:14
  209.4 0.7 copy-start.9
Sparse Core Ops, SparseCore 0:
  75.1 128.8 all-reduce.1
where the time goes:
time: 223 us; the launch traced here: 222 us
  waiting for transfers between devices  86.5 us (39%)
  blocking collectives  41.5 us (19%)
  starting transfers between devices  26.5 us (12%)
  matrix products  23.3 us (10%)
  local copies, waits for them, and re-layouts  18.9 us (8%)
  between operations  14.4 us (6%)
  other arithmetic  11.2 us (5%)
    psum x1, waiting for transfers between devices, per_device(): wsum, bsum = lax.psum((wgrad, bgrad), ('samp', 'sx', 'sy'))  80.6 us
    psum x1, blocking collectives, per_device(): wsum, bsum = lax.psum((wgrad, bgrad), ('samp', 'sx', 'sy'))  41.5 us
    ppermute x4, starting transfers between devices, extended(): before = lax.ppermute(last, axis, up)  21.3 us
    conv_general_dilated x1, matrix products, filter_terms(): lax.conv_general_dilated(padded, delta, (1, 1, 1), ((0, 0), (0, 0), (1, 1...  15.8 us
    concatenate x4, other arithmetic, extended(): shard = jnp.concatenate([before, shard, after], axis=dim)  8.04 us
    concatenate x5, local copies, waits for them, and re-layouts, extended(): shard = jnp.concatenate([before, shard, after], axis=dim)  7.9 us
    unnamed x25, local copies, waits for them, and re-layouts  6.4 us
    ppermute x4, starting transfers between devices, extended(): after = lax.ppermute(initial, axis, down)  5.14 us
  transfers between devices with their start and end apart: 9, of which 5 were waited for; matrix products, arithmetic and copies ran while one was open for 2% of the time, Pallas kernels for 0%

commit v1 on v0

v1 whole, which is shorter than its diff:
```python
import functools
import math

import jax
import jax.numpy as jnp
from jax import lax
from jax.experimental import pallas as pl
from jax.experimental.pallas import tpu as pltpu
from jax.sharding import PartitionSpec as P

MESH = pl.DeviceIdType.MESH
F32 = jnp.float32
BF16 = jnp.bfloat16
DIRS = tuple((dx, dy) for dx in (-1, 0, 1) for dy in (-1, 0, 1) if dx or dy)


def each(count, fn):
    if count <= 8:
        for k in range(1, count):
            fn(k)
    else:
        lax.fori_loop(1, count, lambda k, c: (fn(k), c)[1], 0)


def span(step, size):
    if step > 0:
        return pl.ds(size, 1), pl.ds(0, 1), size
    if step < 0:
        return pl.ds(1, 1), pl.ds(size + 1, 1), 1
    return pl.ds(1, size), pl.ds(1, size), 1


def kernel(
    dims, sizes, chunk, norm,
    vol_ref, w_ref, bias_ref, up_ref,
    act_ref, ig_ref, wg_ref, bg_ref,
    vol_s, up_s, act_s, ig_s, pad, dpad, col, dcol, sd, wt, wb, stage, part, r1, r2, gat,
    hs1, hr1, hs2, hr2, s1, v1, s2, v2, s3, v3,
):
    rows, cols, cin, cout, depth = dims
    n_samp, n_sx, n_sy = sizes
    owners, crows = chunk
    cells = rows * cols
    group = n_sx * n_sy
    me = lax.axis_index("samp")
    ix, iy = lax.axis_index("sx"), lax.axis_index("sy")
    gid = ix * n_sy + iy

    barrier = pltpu.get_barrier_semaphore()

    def greet_samp(k):
        pl.semaphore_signal(barrier, inc=1, device_id={"samp": lax.rem(me + k, n_samp)}, device_id_type=MESH)

    def group_id(k):
        g = lax.rem(gid + k, group)
        return g, {"sx": lax.div(g, n_sy), "sy": lax.rem(g, n_sy)}

    def greet_group(k):
        pl.semaphore_signal(barrier, inc=1, device_id=group_id(k)[1], device_id_type=MESH)

    each(n_samp, greet_samp)
    each(group, greet_group)

    def has(dx, dy):
        ok = None
        for i, step, size in ((ix, dx, n_sx), (iy, dy, n_sy)):
            if step:
                one = (i + 1 < size) if step > 0 else (i > 0)
                ok = one if ok is None else jnp.logical_and(ok, one)
        return ok

    def halo(buf, ss, rs, d):
        dx, dy = DIRS[d]
        sx, tx, _ = span(dx, rows)
        sy, ty, _ = span(dy, cols)
        return pltpu.make_async_remote_copy(
            src_ref=buf.at[sx, sy], dst_ref=buf.at[tx, ty],
            send_sem=ss.at[d], recv_sem=rs.at[d],
            device_id={"sx": ix + dx, "sy": iy + dy}, device_id_type=MESH,
        )

    live = [d for d, (dx, dy) in enumerate(DIRS) if not ((dx and n_sx == 1) or (dy and n_sy == 1))]

    def halo_zero(buf):
        for d, (dx, dy) in enumerate(DIRS):
            _, tx, _ = span(dx, rows)
            _, ty, _ = span(dy, cols)

            def clear():
                v = buf[tx, ty]
                buf[tx, ty] = jnp.zeros_like(v)

            if d in live:
                pl.when(jnp.logical_not(has(-dx, -dy)))(clear)
            else:
                clear()

    def halo_send(buf, ss, rs):
        for d in live:
            pl.when(has(*DIRS[d]))(lambda: halo(buf, ss, rs, d).start())

    def halo_recv(buf, ss, rs):
        for d in live:
            dx, dy = DIRS[d]
            pl.when(has(-dx, -dy))(lambda: halo(buf, ss, rs, d).wait_recv())

    def halo_sent(buf, ss, rs):
        for d in live:
            pl.when(has(*DIRS[d]))(lambda: halo(buf, ss, rs, d).wait_send())

    vol_s[...] = vol_ref[...].astype(F32)
    for x in range(rows):
        for y in range(cols):
            pad[1 + x, 1 + y] = vol_s[pl.ds(x * cols + y, cin, stride=cells), :].astype(BF16)
    pl.semaphore_wait(barrier, n_samp - 1 + group - 1)
    halo_send(pad, hs1, hr1)
    halo_zero(pad)
    halo_zero(dpad)
    for g in range(9):
        for c in range(3):
            block = w_ref[g * 3 + c]
            wt[g * cin:(g + 1) * cin, c * cout:(c + 1) * cout] = block
            wb[c * cin:(c + 1) * cin, g * cout:(g + 1) * cout] = block
    up_s[...] = up_ref[...].astype(F32)
    col[9 * cin:, :] = jnp.ones((16, cells * depth), BF16)
    bias = bias_ref[...]
    lane = lax.broadcasted_iota(jnp.int32, (cout, depth), 1)
    lane_i = lax.broadcasted_iota(jnp.int32, (cin, depth), 1)

    def ahead(v, lanes):
        return jnp.where(lanes < depth - 1, pltpu.roll(v, depth - 1, 1), 0.0)

    def behind(v, lanes):
        return jnp.where(lanes > 0, pltpu.roll(v, 1, 1), 0.0)

    halo_recv(pad, hs1, hr1)
    for x in range(rows):
        for y in range(cols):
            n = x * cols + y
            for a in range(3):
                for b in range(3):
                    g = a * 3 + b
                    col[g * cin:(g + 1) * cin, n * depth:(n + 1) * depth] = pad[x + a, y + b]

    step = 2 if cells % 2 == 0 else 1
    for m in range(0, cells, step):
        rhs = col[0:9 * cin, m * depth:(m + step) * depth]
        out = lax.dot_general(wt[...], rhs, (((0,), (0,)), ((), ())), preferred_element_type=F32)
        for n in range(m, m + step):
            k = (n - m) * depth
            y0, y1, y2 = (out[c * cout:(c + 1) * cout, k:k + depth] for c in range(3))
            pre = behind(y0, lane) + y1 + ahead(y2, lane) + bias
            t = jnp.exp(-jnp.abs(pre))
            soft = jnp.maximum(pre, 0.0) + jnp.log1p(t)
            sig = jnp.where(pre >= 0, 1.0, t) / (1.0 + t)
            act_s[pl.ds(n, cout, stride=cells), :] = 0.3 * pre + 0.7 * soft
            up = up_s[pl.ds(n, cout, stride=cells), :]
            d16 = (up * (0.3 + 0.7 * sig)).astype(BF16)
            dpad[1 + n // cols, 1 + n % cols] = d16
            d = d16.astype(F32)
            sd[0:cout, n * depth:(n + 1) * depth] = ahead(d, lane).astype(BF16)
            sd[cout:2 * cout, n * depth:(n + 1) * depth] = d16
            sd[2 * cout:, n * depth:(n + 1) * depth] = behind(d, lane).astype(BF16)
    halo_send(dpad, hs2, hr2)

    dw = lax.dot_general(col[...], sd[...], (((1,), (1,)), ((), ())), preferred_element_type=F32)
    k9, o2, half = 9 * cin, 2 * cout, 5 * cin
    stage[k9 + half - cin:, :] = jnp.zeros_like(stage[k9 + half - cin:, :])
    stage[0:k9, :] = dw[0:k9, 0:o2]
    stage[k9:k9 + half, 0:cout] = dw[0:half, o2:]
    stage[k9:k9 + k9 - half, cout:] = dw[half:k9, o2:]
    brow = k9 + k9 - half
    stage[brow:brow + 16, cout:] = dw[k9:, cout:o2]
    for q in range(owners):
        part[q] = stage[q * crows:(q + 1) * crows, :].astype(BF16)

    def when(cond, fn, always):
        if always:
            fn()
        else:
            pl.when(cond)(fn)

    every = owners == n_samp
    mine = me < owners

    def rs(src, dst, p):
        return pltpu.make_async_remote_copy(
            src_ref=part.at[src], dst_ref=r1.at[dst], send_sem=s1.at[src], recv_sem=v1.at[dst],
            device_id={"samp": p}, device_id_type=MESH,
        )

    def rs_start(k):
        p = lax.rem(me + k, n_samp)
        when(p < owners, lambda: rs(p, me, p).start(), every)

    def rs_sent(k):
        p = lax.rem(me + k, n_samp)
        when(p < owners, lambda: rs(p, me, p).wait_send(), every)

    each(n_samp, rs_start)
    act_ref[...] = act_s[...].astype(BF16)

    halo_recv(dpad, hs2, hr2)
    for x in range(rows):
        for y in range(cols):
            n = x * cols + y
            for a in range(3):
                for b in range(3):
                    g = a * 3 + b
                    dcol[g * cout:(g + 1) * cout, n * depth:(n + 1) * depth] = dpad[x + 2 - a, y + 2 - b]

    def backward(lo, hi):
        for m in range(lo, hi, step):
            out = jnp.dot(wb[...], dcol[:, m * depth:(m + step) * depth], preferred_element_type=F32)
            for n in range(m, m + step):
                k = (n - m) * depth
                u0, u1, u2 = (out[c * cin:(c + 1) * cin, k:k + depth] for c in range(3))
                ig_s[pl.ds(n, cin, stride=cells), :] = ahead(u0, lane_i) + u1 + behind(u2, lane_i)

    def gs(k):
        g, dev = group_id(k)
        return pltpu.make_async_remote_copy(
            src_ref=r2.at[gid], dst_ref=r2.at[gid], send_sem=s2.at[g], recv_sem=v2.at[gid],
            device_id=dev, device_id_type=MESH,
        )

    def gs_from(k):
        g, dev = group_id(k)
        return pltpu.make_async_remote_copy(
            src_ref=r2.at[g], dst_ref=r2.at[g], send_sem=s2.at[g], recv_sem=v2.at[g],
            device_id=dev, device_id_type=MESH,
        )

    def reduce_own():
        each(n_samp, lambda k: rs(0, lax.rem(me + k, n_samp), 0).wait_recv())
        r1[me] = part[me]
        total = lax.fori_loop(1, n_samp, lambda j, t: t + r1[j].astype(F32), r1[0].astype(F32))
        r2[gid] = total.astype(BF16)
        each(group, lambda k: gs(k).start())

    def ag(slot, p, sem):
        return pltpu.make_async_remote_copy(
            src_ref=gat.at[slot], dst_ref=gat.at[slot], send_sem=s3.at[sem], recv_sem=v3.at[slot],
            device_id={"samp": p}, device_id_type=MESH,
        )

    def ag_start(k):
        p = lax.rem(me + k, n_samp)
        ag(me, p, p).start()

    def gather_own():
        each(group, lambda k: gs_from(k).wait_recv())
        total = r2[0].astype(F32)
        for j in range(1, group):
            total = total + r2[j].astype(F32)
        gat[me] = total.astype(BF16)
        each(n_samp, ag_start)

    backward(0, cells)
    when(mine, reduce_own, every)
    ig_ref[...] = ig_s[...].astype(BF16)
    when(mine, gather_own, every)

    def ag_recv(k):
        p = lax.rem(me + k, n_samp)
        when(p < owners, lambda: ag(p, p, p).wait_recv(), every)

    each(n_samp, ag_recv)
    for q in range(owners):
        stage[q * crows:(q + 1) * crows, :] = gat[q].astype(F32) * norm
    for g in range(9):
        lo = g * cin
        wg_ref[g * 3] = stage[lo:lo + cin, 0:cout]
        wg_ref[g * 3 + 1] = stage[lo:lo + cin, cout:]
        if g < 5:
            wg_ref[g * 3 + 2] = stage[k9 + lo:k9 + lo + cin, 0:cout]
        else:
            wg_ref[g * 3 + 2] = stage[k9 + lo - half:k9 + lo - half + cin, cout:]
    bg_ref[...] = stage[brow:brow + 1, cout:]

    halo_sent(pad, hs1, hr1)
    halo_sent(dpad, hs2, hr2)
    each(n_samp, rs_sent)

    def own_sent():
        each(group, lambda k: gs(k).wait_send())
        each(n_samp, lambda k: ag(me, lax.rem(me + k, n_samp), lax.rem(me + k, n_samp)).wait_send())

    when(mine, own_sent, every)


def per_device(volume, kern, bias, upstream):
    samples, cin, rows, cols, depth = volume.shape
    cout = kern.shape[0]
    sizes = tuple(lax.axis_size(a) for a in ("samp", "sx", "sy"))
    cells = rows * cols
    packed = 14 * cin
    owners = min(sizes[0], 7)
    crows = -(-packed // (owners * 16)) * 16
    norm = 1.0 / math.sqrt(sizes[0] * samples * sizes[1] * sizes[2] * cells * depth)
    group = sizes[1] * sizes[2]
    dma = pltpu.SemaphoreType.DMA
    v = pltpu.VMEM
    whole = pl.BlockSpec(memory_space=pltpu.VMEM)
    w = kern.transpose(2, 3, 4, 1, 0).reshape(27, cin, cout)
    act, ig, wg, bg = pl.pallas_call(
        functools.partial(kernel, (rows, cols, cin, cout, depth), sizes, (owners, crows), norm),
        out_shape=(
            jax.ShapeDtypeStruct((cout * cells, depth), BF16),
            jax.ShapeDtypeStruct((cin * cells, depth), BF16),
            jax.ShapeDtypeStruct((27, cin, cout), F32),
            jax.ShapeDtypeStruct((1, cout), F32),
        ),
        in_specs=[whole] * 4,
        out_specs=[whole] * 4,
        scratch_shapes=[
            v((cin * cells, depth), F32), v((cout * cells, depth), F32),
            v((cout * cells, depth), F32), v((cin * cells, depth), F32),
            v((rows + 2, cols + 2, cin, depth), BF16), v((rows + 2, cols + 2, cout, depth), BF16),
            v((9 * cin + 16, cells * depth), BF16), v((9 * cout, cells * depth), BF16),
            v((3 * cout, cells * depth), BF16),
            v((9 * cin, 3 * cout), BF16), v((3 * cin, 9 * cout), BF16),
            v((owners * crows, 2 * cout), F32), v((owners, crows, 2 * cout), BF16),
            v((sizes[0], crows, 2 * cout), BF16), v((group, crows, 2 * cout), BF16),
            v((owners, crows, 2 * cout), BF16),
            dma((8,)), dma((8,)), dma((8,)), dma((8,)),
            dma((owners,)), dma((sizes[0],)), dma((group,)), dma((group,)),
            dma((sizes[0],)), dma((owners,)),
        ],
        compiler_params=pltpu.CompilerParams(
            collective_id=0, has_side_effects=True, vmem_limit_bytes=40 << 20
        ),
    )(
        volume.reshape(cin * cells, depth), w, bias.reshape(cout, 1), upstream.reshape(cout * cells, depth)
    )
    shape = (samples, -1, rows, cols, depth)
    filt = wg.reshape(3, 3, 3, cin, cout).transpose(4, 3, 0, 1, 2)
    return act.reshape(shape), ig.reshape(shape), filt, bg.reshape(cout)


def solution(mesh):
    block = P("samp", None, "sx", "sy", None)
    return jax.shard_map(
        per_device, mesh=mesh, in_specs=(block, P(), P(), block),
        out_specs=(block, block, P(), P()), check_vma=False,
    )
```

time: 223 us -> 35.6 us (0.16)
  waiting for transfers between devices: 86.5 us -> 0 us
  blocking collectives: 41.5 us -> 0 us
  Pallas kernels: 0 us -> 28.6 us
  starting transfers between devices: 26.5 us -> 0 us
  matrix products: 23.3 us -> 0 us
  between operations: 14.4 us -> 0.65 us
  local copies, waits for them, and re-layouts: 18.9 us -> 6.16 us
  other arithmetic: 11.2 us -> 0 us
    psum x1 -> x0, waiting for transfers between devices: 80.6 us -> none  [per_device(): wsum, bsum = lax.psum((wgrad, bgrad), ('samp', 'sx', 'sy'))]
    psum x1 -> x0, blocking collectives: 41.5 us -> none  [per_device(): wsum, bsum = lax.psum((wgrad, bgrad), ('samp', 'sx', 'sy'))]
    pallas_call x0 -> x1, Pallas kernels: none -> 28.6 us  [per_device(): pl.pallas_call(functools.partial(kernel, (rows, cols, cin, cout, depth),...]
    ppermute x8 -> x0, starting transfers between devices: 26.5 us -> none  [the longest x4 21.3 us: extended(): before = lax.ppermute(last, axis, up)]
    conv_general_dilated x3 -> x0, matrix products: 23.3 us -> none  [the longest x1 15.8 us: filter_terms(): lax.conv_general_dilated(padded, delta, (1, 1, 1), ((0, 0), (0, 0), (1, 1...]
    concatenate x4 -> x0, other arithmetic: 8.04 us -> none  [extended(): shard = jnp.concatenate([before, shard, after], axis=dim)]
    concatenate x5 -> x0, local copies, waits for them, and re-layouts: 7.9 us -> none  [extended(): shard = jnp.concatenate([before, shard, after], axis=dim)]
    ppermute x8 -> x0, waiting for transfers between devices: 5.96 us -> none  [the longest x4 3.07 us: extended(): after = lax.ppermute(initial, axis, down)]
  transfers between devices with their start and end apart: 9 -> 0, of which waited for: 5 -> 0; matrix products, arithmetic and copies ran while one was open for 2% -> 0% of each run, Pallas kernels for 0% -> 0%
where the time goes in v1:
time: 35.6 us; the launch traced here: 35.4 us
  Pallas kernels  28.6 us (80%)
  local copies, waits for them, and re-layouts  6.16 us (17%)
  between operations  0.65 us (2%)
    pallas_call x1, Pallas kernels, per_device(): pl.pallas_call(functools.partial(kernel, (rows, cols, cin, cout, depth),...  28.6 us
    unnamed x12, local copies, waits for them, and re-layouts  6.07 us

profile of v1, /device:TPU:0, one launch (start us, length us, event | category | flops | bytes accessed | tf_op | source)
XLA Modules:
  0.0 35.4 jit_solution(1687672230364573903)
XLA Ops:
  0.6 0.0 copy-start.3
  0.6 0.6 %copy-done.3 = f32[64]{0:T(128)S(1)} copy-done((f32[64]{0:T(128)S(1)}, f32[64]{0:T(128)}, u32[]{:S(2)}) %copy-start.3) | copy-done | bytes 280
  1.3 0.1 copy.8.bias_ref
  1.4 0.0 copy-start
  1.4 0.9 %copy-done = bf16[1,64,2,8,128]{4,3,2,1,0:T(8,128)(2,1)S(1)} copy-done((bf16[1,64,2,8,128]{4,3,2,1,0:T(8,128)(2,1)S(1)}, bf16[1,64,2,8,128]{4,3,2,1,0:T(8,128)(2,1)}, u32[]{:S(2)}) %copy-start) | copy-done | bytes 262168
  2.3 0.0 copy-start.1
  2.3 0.9 %copy-done.1 = bf16[64,32,3,3,3]{0,1,4,3,2:T(8,128)(2,1)S(1)} copy-done((bf16[64,32,3,3,3]{0,1,4,3,2:T(8,128)(2,1)S(1)}, bf16[64,32,3,3,3]{0,1,4,3,2:T(8,128)(2,1)}, u32[]{:S(2)}) %copy-start.1) | copy-done | bytes 110616
  3.3 0.0 copy-start.2
  3.3 0.9 %copy-done.2 = bf16[1,32,2,8,128]{4,3,2,1,0:T(8,128)(2,1)S(1)} copy-done((bf16[1,32,2,8,128]{4,3,2,1,0:T(8,128)(2,1)S(1)}, bf16[1,32,2,8,128]{4,3,2,1,0:T(8,128)(2,1)}, u32[]{:S(2)}) %copy-start.2) | copy-done | bytes 131096
  4.2 28.6 %shard_map.75 = (bf16[1024,128]{1,0:T(8,128)(2,1)S(1)}, bf16[512,128]{1,0:T(8,128)(2,1)S(1)}, f32[27,32,64]{2,1,0:T(8,128)S(1)}, f32[1,64]{1,0:T(1,128)S(1)}) custom-call(bf16[512,128]{1,0:T(8,128)(2,1)S(1)} %bitcast.16, bf16[27,32,64]{2,1,0:T(8,128)(2,1)S(1)} %bitcast.15, f32[64,1]{1,0:T(8,128)S(1)} %copy.8.bias_ref, bf16[1024,128]{1,0:T(8,128)(2,1)S(1)} %bitcast.13), custom_call_target="tpu_custom_call" | custom-call | tf_op jit(solution)/shard_map/pallas_call | solution.py:306
  32.8 0.7 %copy.13 = bf16[1,64,2,8,128]{4,3,2,1,0:T(8,128)(2,1)} copy(bf16[1,64,2,8,128]{4,3,2,1,0:T(8,128)(2,1)S(1)} %bitcast.14) | data formatting | bytes 524288
  33.5 0.7 %copy.14 = bf16[1,32,2,8,128]{4,3,2,1,0:T(8,128)(2,1)} copy(bf16[1,32,2,8,128]{4,3,2,1,0:T(8,128)(2,1)S(1)} %bitcast.17) | data formatting | bytes 262144
  34.2 0.8 %copy.15 = f32[64,32,3,3,3]{0,1,4,3,2:T(8,128)} copy(f32[64,32,3,3,3]{0,1,4,3,2:T(8,128)S(1)} %bitcast.12) | data formatting | bytes 442368
  34.9 0.5 %copy.16 = f32[64]{0:T(128)} copy(f32[64]{0:T(128)S(1)} %bitcast.18) | data formatting | bytes 512
Async XLA Ops:
  0.6 0.7 %copy-start.3 = (f32[64]{0:T(128)S(1)}, f32[64]{0:T(128)}, u32[]{:S(2)}) copy-start(f32[64]{0:T(128)} %param.6) | copy-start | bytes 772
  1.4 0.9 %copy-start = (bf16[1,64,2,8,128]{4,3,2,1,0:T(8,128)(2,1)S(1)}, bf16[1,64,2,8,128]{4,3,2,1,0:T(8,128)(2,1)}, u32[]{:S(2)}) copy-start(bf16[1,64,2,8,128]{4,3,2,1,0:T(8,128)(2,1)} %param.7) | copy-start | bytes 786436
  2.3 0.9 %copy-start.1 = (bf16[64,32,3,3,3]{0,1,4,3,2:T(8,128)(2,1)S(1)}, bf16[64,32,3,3,3]{0,1,4,3,2:T(8,128)(2,1)}, u32[]{:S(2)}) copy-start(bf16[64,32,3,3,3]{0,1,4,3,2:T(8,128)(2,1)} %param.5) | copy-start | bytes 331780
  3.3 0.9 %copy-start.2 = (bf16[1,32,2,8,128]{4,3,2,1,0:T(8,128)(2,1)S(1)}, bf16[1,32,2,8,128]{4,3,2,1,0:T(8,128)(2,1)}, u32[]{:S(2)}) copy-start(bf16[1,32,2,8,128]{4,3,2,1,0:T(8,128)(2,1)} %param.4) | copy-start | bytes 393220

commit v2 on v1

--- a/solution.py
+++ b/solution.py
@@ -24,18 +24,27 @@
 
 def span(step, size):
     if step > 0:
-        return pl.ds(size, 1), pl.ds(0, 1), size
+        return pl.ds(size, 1), pl.ds(0, 1), pl.ds(size + 1, 1)
     if step < 0:
-        return pl.ds(1, 1), pl.ds(size + 1, 1), 1
-    return pl.ds(1, size), pl.ds(1, size), 1
+        return pl.ds(1, 1), pl.ds(size + 1, 1), pl.ds(0, 1)
+    return pl.ds(1, size), pl.ds(1, size), pl.ds(1, size)
+
+
+def taps(step):
+    return {1: (2,), -1: (0,), 0: (0, 1, 2)}[step]
+
+
+def places(step, size):
+    return {1: (size + 1,), -1: (0,), 0: tuple(range(1, size + 1))}[step]
 
 
 def kernel(
     dims, sizes, chunk, norm,
+    vol_hbm, w_hbm, bias_hbm, up_hbm,
+    act_ref, ig_ref, gat,
     vol_ref, w_ref, bias_ref, up_ref,
-    act_ref, ig_ref, wg_ref, bg_ref,
-    vol_s, up_s, act_s, ig_s, pad, dpad, col, dcol, sd, wt, wb, stage, part, r1, r2, gat,
-    hs1, hr1, hs2, hr2, s1, v1, s2, v2, s3, v3,
+    vol_s, up_s, act_s, ig_s, pad, dpad, hout, hin, col, dcol, sd, wt, wtt, wb, wbs, stage, part, r1, r2,
+    ls, hs1, hr1, hs2, hr2, s1, v1, s2, v2, s3, v3,
 ):
     rows, cols, cin, cout, depth = dims
     n_samp, n_sx, n_sy = sizes
@@ -46,6 +55,14 @@
     ix, iy = lax.axis_index("sx"), lax.axis_index("sy")
     gid = ix * n_sy + iy
 
+    loads = [
+        pltpu.make_async_copy(src, dst, ls.at[i])
+        for i, (src, dst) in enumerate(
+            ((vol_hbm, vol_ref), (w_hbm, w_ref), (bias_hbm, bias_ref), (up_hbm, up_ref))
+        )
+    ]
+    for load in loads:
+        load.start()
     barrier = pltpu.get_barrier_semaphore()
 
     def greet_samp(k):
@@ -71,10 +88,11 @@
 
     def halo(buf, ss, rs, d):
         dx, dy = DIRS[d]
-        sx, tx, _ = span(dx, rows)
-        sy, ty, _ = span(dy, cols)
+        sx, tx, ox = span(dx, rows)
+        sy, ty, oy = span(dy, cols)
+        src = buf.at[sx, sy] if buf is pad else hout.at[ox, oy]
         return pltpu.make_async_remote_copy(
-            src_ref=buf.at[sx, sy], dst_ref=buf.at[tx, ty],
+            src_ref=src, dst_ref=buf.at[tx, ty],
             send_sem=ss.at[d], recv_sem=rs.at[d],
             device_id={"sx": ix + dx, "sy": iy + dy}, device_id_type=MESH,
         )
@@ -108,6 +126,7 @@
         for d in live:
             pl.when(has(*DIRS[d]))(lambda: halo(buf, ss, rs, d).wait_send())
 
+    loads[0].wait()
     vol_s[...] = vol_ref[...].astype(F32)
     for x in range(rows):
         for y in range(cols):
@@ -115,15 +134,25 @@
     pl.semaphore_wait(barrier, n_samp - 1 + group - 1)
     halo_send(pad, hs1, hr1)
     halo_zero(pad)
-    halo_zero(dpad)
+    halo_zero(hin)
+    for x in (0, rows + 1):
+        dpad[x] = jnp.zeros((cols + 2, cout, depth), BF16)
+    for x in range(1, rows + 1):
+        for y in (0, cols + 1):
+            dpad[x, y] = jnp.zeros((cout, depth), BF16)
+    for load in loads[1:]:
+        load.wait()
     for g in range(9):
         for c in range(3):
             block = w_ref[g * 3 + c]
             wt[g * cin:(g + 1) * cin, c * cout:(c + 1) * cout] = block
             wb[c * cin:(c + 1) * cin, g * cout:(g + 1) * cout] = block
+            wbs[g, c * cin:(c + 1) * cin, :] = block
+    wtt[...] = wt[...].T
     up_s[...] = up_ref[...].astype(F32)
     col[9 * cin:, :] = jnp.ones((16, cells * depth), BF16)
-    bias = bias_ref[...]
+    eye = lax.broadcasted_iota(jnp.int32, (cout, cout), 0) == lax.broadcasted_iota(jnp.int32, (cout, cout), 1)
+    bias = jnp.sum(jnp.where(eye, bias_ref[...], 0.0), axis=1, keepdims=True)
     lane = lax.broadcasted_iota(jnp.int32, (cout, depth), 1)
     lane_i = lax.broadcasted_iota(jnp.int32, (cin, depth), 1)
 
@@ -145,14 +174,15 @@
     step = 2 if cells % 2 == 0 else 1
     for m in range(0, cells, step):
         rhs = col[0:9 * cin, m * depth:(m + step) * depth]
-        out = lax.dot_general(wt[...], rhs, (((0,), (0,)), ((), ())), preferred_element_type=F32)
+        out = jnp.dot(wtt[...], rhs, preferred_element_type=F32)
         for n in range(m, m + step):
             k = (n - m) * depth
             y0, y1, y2 = (out[c * cout:(c + 1) * cout, k:k + depth] for c in range(3))
             pre = behind(y0, lane) + y1 + ahead(y2, lane) + bias
             t = jnp.exp(-jnp.abs(pre))
-            soft = jnp.maximum(pre, 0.0) + jnp.log1p(t)
-            sig = jnp.where(pre >= 0, 1.0, t) / (1.0 + t)
+            one = 1.0 + t
+            soft = jnp.maximum(pre, 0.0) + jnp.log(one)
+            sig = jnp.where(pre >= 0, 1.0, t) / one
             act_s[pl.ds(n, cout, stride=cells), :] = 0.3 * pre + 0.7 * soft
             up = up_s[pl.ds(n, cout, stride=cells), :]
             d16 = (up * (0.3 + 0.7 * sig)).astype(BF16)
@@ -161,7 +191,6 @@
             sd[0:cout, n * depth:(n + 1) * depth] = ahead(d, lane).astype(BF16)
             sd[cout:2 * cout, n * depth:(n + 1) * depth] = d16
             sd[2 * cout:, n * depth:(n + 1) * depth] = behind(d, lane).astype(BF16)
-    halo_send(dpad, hs2, hr2)
 
     dw = lax.dot_general(col[...], sd[...], (((1,), (1,)), ((), ())), preferred_element_type=F32)
     k9, o2, half = 9 * cin, 2 * cout, 5 * cin
@@ -198,9 +227,26 @@
         when(p < owners, lambda: rs(p, me, p).wait_send(), every)
 
     each(n_samp, rs_start)
+
+    def outside(d):
+        dx, dy = DIRS[d]
+        spots = [(x, y) for x in places(dx, rows) for y in places(dy, cols)]
+        for m in range(0, len(spots), 2):
+            pair = spots[m:m + 2]
+            out = None
+            for a in taps(dx):
+                for b in taps(dy):
+                    rhs = jnp.concatenate([dpad[x + 1 - a, y + 1 - b] for x, y in pair], axis=1)
+                    term = jnp.dot(wbs[a * 3 + b], rhs, preferred_element_type=F32)
+                    out = term if out is None else out + term
+            for n, (x, y) in enumerate(pair):
+                u0, u1, u2 = (out[c * cin:(c + 1) * cin, n * depth:(n + 1) * depth] for c in range(3))
+                hout[x, y] = (ahead(u0, lane_i) + u1 + behind(u2, lane_i)).astype(BF16)
+        halo(hin, hs2, hr2, d).start()
+
+    for d in live:
+        pl.when(has(*DIRS[d]))(lambda: outside(d))
     act_ref[...] = act_s[...].astype(BF16)
-
-    halo_recv(dpad, hs2, hr2)
     for x in range(rows):
         for y in range(cols):
             n = x * cols + y
@@ -258,6 +304,20 @@
 
     backward(0, cells)
     when(mine, reduce_own, every)
+    halo_recv(hin, hs2, hr2)
+    for x in range(1, rows + 1):
+        for y in range(1, cols + 1):
+            spots = []
+            for dx in (-1, 0, 1):
+                for dy in (-1, 0, 1):
+                    if (dx or dy) and (not dx or x == (1 if dx < 0 else rows)) and (not dy or y == (1 if dy < 0 else cols)):
+                        spots.append((x + dx, y + dy))
+            if spots:
+                at = pl.ds((x - 1) * cols + y - 1, cin, stride=cells)
+                total = ig_s[at, :]
+                for spot in spots:
+                    total = total + hin[spot].astype(F32)
+                ig_s[at, :] = total
     ig_ref[...] = ig_s[...].astype(BF16)
     when(mine, gather_own, every)
 
@@ -266,6 +326,28 @@
         when(p < owners, lambda: ag(p, p, p).wait_recv(), every)
 
     each(n_samp, ag_recv)
+    halo_sent(pad, hs1, hr1)
+    halo_sent(hin, hs2, hr2)
+    each(n_samp, rs_sent)
+
+    def own_sent():
+        each(group, lambda k: gs(k).wait_send())
+        each(n_samp, lambda k: ag(me, lax.rem(me + k, n_samp), lax.rem(me + k, n_samp)).wait_send())
+
+    when(mine, own_sent, every)
+
+
+def finish(norm, cin, cout, act_ref, ig_ref, gat, act_hbm, ig_hbm, wg_hbm, bg_hbm, stage, wg_ref, bg_ref, sem):
+    copies = [
+        pltpu.make_async_copy(src, dst, sem.at[i])
+        for i, (src, dst) in enumerate(
+            ((act_ref, act_hbm), (ig_ref, ig_hbm), (wg_ref, wg_hbm), (bg_ref, bg_hbm))
+        )
+    ]
+    copies[0].start()
+    copies[1].start()
+    owners, crows, _ = gat.shape
+    k9, half = 9 * cin, 5 * cin
     for q in range(owners):
         stage[q * crows:(q + 1) * crows, :] = gat[q].astype(F32) * norm
     for g in range(9):
@@ -276,17 +358,12 @@
             wg_ref[g * 3 + 2] = stage[k9 + lo:k9 + lo + cin, 0:cout]
         else:
             wg_ref[g * 3 + 2] = stage[k9 + lo - half:k9 + lo - half + cin, cout:]
+    brow = k9 + k9 - half
     bg_ref[...] = stage[brow:brow + 1, cout:]
-
-    halo_sent(pad, hs1, hr1)
-    halo_sent(dpad, hs2, hr2)
-    each(n_samp, rs_sent)
-
-    def own_sent():
-        each(group, lambda k: gs(k).wait_send())
-        each(n_samp, lambda k: ag(me, lax.rem(me + k, n_samp), lax.rem(me + k, n_samp)).wait_send())
-
-    when(mine, own_sent, every)
+    copies[2].start()
+    copies[3].start()
+    for copy in copies:
+        copy.wait()
 
 
 def per_device(volume, kern, bias, upstream):
@@ -303,27 +380,29 @@
     v = pltpu.VMEM
     whole = pl.BlockSpec(memory_space=pltpu.VMEM)
     w = kern.transpose(2, 3, 4, 1, 0).reshape(27, cin, cout)
-    act, ig, wg, bg = pl.pallas_call(
+    hbm = pl.BlockSpec(memory_space=pltpu.HBM)
+    act_out = jax.ShapeDtypeStruct((cout * cells, depth), BF16)
+    ig_out = jax.ShapeDtypeStruct((cin * cells, depth), BF16)
+    wg_out = jax.ShapeDtypeStruct((27, cin, cout), F32)
+    bg_out = jax.ShapeDtypeStruct((1, cout), F32)
+    act, ig, gat = pl.pallas_call(
         functools.partial(kernel, (rows, cols, cin, cout, depth), sizes, (owners, crows), norm),
-        out_shape=(
-            jax.ShapeDtypeStruct((cout * cells, depth), BF16),
-            jax.ShapeDtypeStruct((cin * cells, depth), BF16),
-            jax.ShapeDtypeStruct((27, cin, cout), F32),
-            jax.ShapeDtypeStruct((1, cout), F32),
-        ),
-        in_specs=[whole] * 4,
-        out_specs=[whole] * 4,
+        out_shape=(act_out, ig_out, jax.ShapeDtypeStruct((owners, crows, 2 * cout), BF16)),
+        in_specs=[hbm] * 4,
+        out_specs=[whole] * 3,
         scratch_shapes=[
+            v((cin * cells, depth), BF16), v((27, cin, cout), BF16), v((1, cout), F32), v((cout * cells, depth), BF16),
             v((cin * cells, depth), F32), v((cout * cells, depth), F32),
             v((cout * cells, depth), F32), v((cin * cells, depth), F32),
             v((rows + 2, cols + 2, cin, depth), BF16), v((rows + 2, cols + 2, cout, depth), BF16),
+            v((rows + 2, cols + 2, cin, depth), BF16), v((rows + 2, cols + 2, cin, depth), BF16),
             v((9 * cin + 16, cells * depth), BF16), v((9 * cout, cells * depth), BF16),
             v((3 * cout, cells * depth), BF16),
-            v((9 * cin, 3 * cout), BF16), v((3 * cin, 9 * cout), BF16),
+            v((9 * cin, 3 * cout), BF16), v((3 * cout, 9 * cin), BF16), v((3 * cin, 9 * cout), BF16),
+            v((9, 3 * cin, cout), BF16),
             v((owners * crows, 2 * cout), F32), v((owners, crows, 2 * cout), BF16),
             v((sizes[0], crows, 2 * cout), BF16), v((group, crows, 2 * cout), BF16),
-            v((owners, crows, 2 * cout), BF16),
-            dma((8,)), dma((8,)), dma((8,)), dma((8,)),
+            dma((4,)), dma((8,)), dma((8,)), dma((8,)), dma((8,)),
             dma((owners,)), dma((sizes[0],)), dma((group,)), dma((group,)),
             dma((sizes[0],)), dma((owners,)),
         ],
@@ -331,8 +410,21 @@
             collective_id=0, has_side_effects=True, vmem_limit_bytes=40 << 20
         ),
     )(
-        volume.reshape(cin * cells, depth), w, bias.reshape(cout, 1), upstream.reshape(cout * cells, depth)
+        *(
+            pltpu.with_memory_space_constraint(x, pltpu.HBM)
+            for x in (
+                volume.reshape(cin * cells, depth), w, bias.reshape(1, cout), upstream.reshape(cout * cells, depth)
+            )
+        )
     )
+    act, ig, wg, bg = pl.pallas_call(
+        functools.partial(finish, norm, cin, cout),
+        out_shape=(act_out, ig_out, wg_out, bg_out),
+        in_specs=[whole] * 3,
+        out_specs=[hbm] * 4,
+        scratch_shapes=[v((owners * crows, 2 * cout), F32), v((27, cin, cout), F32), v((1, cout), F32), dma((4,))],
+        compiler_params=pltpu.CompilerParams(vmem_limit_bytes=16 << 20),
+    )(act, ig, gat)
     shape = (samples, -1, rows, cols, depth)
     filt = wg.reshape(3, 3, 3, cin, cout).transpose(4, 3, 0, 1, 2)
     return act.reshape(shape), ig.reshape(shape), filt, bg.reshape(cout)

time: 35.6 us -> 25.3 us (0.71)
  local copies, waits for them, and re-layouts: 6.16 us -> 0 us
  Pallas kernels: 28.6 us -> 24.5 us
    unnamed x12 -> x0, local copies, waits for them, and re-layouts: 6.07 us -> none
    pallas_call x1, Pallas kernels: 28.6 us -> 23.6 us  [per_device(): pl.pallas_call(functools.partial(kernel, (rows, cols, cin, cout, depth),...]
    pallas_call x0 -> x1, Pallas kernels: none -> 0.93 us  [per_device(): pl.pallas_call(functools.partial(finish, norm, cin, cout), out_shape=(act...]
where the time goes in v2:
time: 25.3 us; the launch traced here: 25.1 us
  Pallas kernels  24.5 us (97%)
  between operations  0.64 us (3%)
    pallas_call x1, Pallas kernels, per_device(): pl.pallas_call(functools.partial(kernel, (rows, cols, cin, cout, depth),...  23.6 us
    pallas_call x1, Pallas kernels, per_device(): pl.pallas_call(functools.partial(finish, norm, cin, cout), out_shape=(act...  0.93 us

profile of v2, /device:TPU:0, one launch (start us, length us, event | category | flops | bytes accessed | tf_op | source)
XLA Modules:
  0.0 25.1 jit_solution(11934575560836073189)
XLA Ops:
  0.6 23.6 %shard_map.75 = (bf16[1024,128]{1,0:T(8,128)(2,1)S(1)}, bf16[512,128]{1,0:T(8,128)(2,1)S(1)}, bf16[7,64,128]{2,1,0:T(8,128)(2,1)S(1)}) custom-call(bf16[512,128]{1,0:T(8,128)(2,1)} %bitcast.14, bf16[27,32,64]{2,1,0:T(8,128)(2,1)} %bitcast.13, f32[1,64]{1,0:T(1,128)} %bitcast.15, bf16[1024,128]{1,0:T(8,128)(2,1)} %bitcast.12), custom_call_target="tpu_custom_call" | custom-call | tf_op jit(solution)/shard_map/pallas_call | solution.py:388
  24.2 0.9 %shard_map.76 = (bf16[1024,128]{1,0:T(8,128)(2,1)}, bf16[512,128]{1,0:T(8,128)(2,1)}, f32[27,32,64]{2,1,0:T(8,128)}, f32[1,64]{1,0:T(1,128)}) custom-call(bf16[1024,128]{1,0:T(8,128)(2,1)S(1)} %get-tuple-element.11.act_ref, bf16[512,128]{1,0:T(8,128)(2,1)S(1)} %get-tuple-element.12.ig_ref, bf16[7,64,128]{2,1,0:T(8,128)(2,1)S(1)} %get-tuple-element.13.gat), custom_call_target="tpu_custom_call" | custom-call | tf_op jit(solution)/shard_map/pallas_call | solution.py:420

commit v3 on v2

--- a/solution.py
+++ b/solution.py
@@ -43,7 +43,7 @@
     vol_hbm, w_hbm, bias_hbm, up_hbm,
     act_ref, ig_ref, gat,
     vol_ref, w_ref, bias_ref, up_ref,
-    vol_s, up_s, act_s, ig_s, pad, dpad, hout, hin, col, dcol, sd, wt, wtt, wb, wbs, stage, part, r1, r2,
+    vol_s, up_s, act_s, ig_s, pad, dpad, hout, hin, col, ys, dcol, sd, wt, wtt, wb, wbs, stage, part, r1, r2,
     ls, hs1, hr1, hs2, hr2, s1, v1, s2, v2, s3, v3,
 ):
     rows, cols, cin, cout, depth = dims
@@ -86,14 +86,19 @@
                 ok = one if ok is None else jnp.logical_and(ok, one)
         return ok
 
-    def halo(buf, ss, rs, d):
+    half = cols // 2 if cols % 4 == 0 else cols
+
+    def halo(buf, ss, rs, d, piece=0):
         dx, dy = DIRS[d]
         sx, tx, ox = span(dx, rows)
         sy, ty, oy = span(dy, cols)
+        if buf is pad and not dy and half < cols:
+            sy = ty = pl.ds(half + 2, cols - half - 1) if piece else pl.ds(1, half + 1)
+        sem = d + 8 * piece
         src = buf.at[sx, sy] if buf is pad else hout.at[ox, oy]
         return pltpu.make_async_remote_copy(
             src_ref=src, dst_ref=buf.at[tx, ty],
-            send_sem=ss.at[d], recv_sem=rs.at[d],
+            send_sem=ss.at[sem], recv_sem=rs.at[sem],
             device_id={"sx": ix + dx, "sy": iy + dy}, device_id_type=MESH,
         )
 
@@ -113,18 +118,23 @@
             else:
                 clear()
 
+    late = [d for d in live if not DIRS[d][1]] if half < cols else []
+    near = sorted(live, key=lambda d: (d in late, DIRS[d][1] == 0))
+
     def halo_send(buf, ss, rs):
-        for d in live:
+        for d in near:
             pl.when(has(*DIRS[d]))(lambda: halo(buf, ss, rs, d).start())
-
-    def halo_recv(buf, ss, rs):
-        for d in live:
+        for d in late:
+            pl.when(has(*DIRS[d]))(lambda: halo(buf, ss, rs, d, 1).start())
+
+    def halo_recv(buf, ss, rs, which, piece=0):
+        for d in which:
             dx, dy = DIRS[d]
-            pl.when(has(-dx, -dy))(lambda: halo(buf, ss, rs, d).wait_recv())
-
-    def halo_sent(buf, ss, rs):
-        for d in live:
-            pl.when(has(*DIRS[d]))(lambda: halo(buf, ss, rs, d).wait_send())
+            pl.when(has(-dx, -dy))(lambda: halo(buf, ss, rs, d, piece).wait_recv())
+
+    def halo_sent(buf, ss, rs, which, piece=0):
+        for d in which:
+            pl.when(has(*DIRS[d]))(lambda: halo(buf, ss, rs, d, piece).wait_send())
 
     loads[0].wait()
     vol_s[...] = vol_ref[...].astype(F32)
@@ -153,7 +163,6 @@
     col[9 * cin:, :] = jnp.ones((16, cells * depth), BF16)
     eye = lax.broadcasted_iota(jnp.int32, (cout, cout), 0) == lax.broadcasted_iota(jnp.int32, (cout, cout), 1)
     bias = jnp.sum(jnp.where(eye, bias_ref[...], 0.0), axis=1, keepdims=True)
-    lane = lax.broadcasted_iota(jnp.int32, (cout, depth), 1)
     lane_i = lax.broadcasted_iota(jnp.int32, (cin, depth), 1)
 
     def ahead(v, lanes):
@@ -162,43 +171,64 @@
     def behind(v, lanes):
         return jnp.where(lanes > 0, pltpu.roll(v, 1, 1), 0.0)
 
-    halo_recv(pad, hs1, hr1)
-    for x in range(rows):
-        for y in range(cols):
-            n = x * cols + y
-            for a in range(3):
-                for b in range(3):
-                    g = a * 3 + b
-                    col[g * cin:(g + 1) * cin, n * depth:(n + 1) * depth] = pad[x + a, y + b]
-
-    step = 2 if cells % 2 == 0 else 1
-    for m in range(0, cells, step):
-        rhs = col[0:9 * cin, m * depth:(m + step) * depth]
-        out = jnp.dot(wtt[...], rhs, preferred_element_type=F32)
-        for n in range(m, m + step):
-            k = (n - m) * depth
-            y0, y1, y2 = (out[c * cout:(c + 1) * cout, k:k + depth] for c in range(3))
-            pre = behind(y0, lane) + y1 + ahead(y2, lane) + bias
-            t = jnp.exp(-jnp.abs(pre))
-            one = 1.0 + t
-            soft = jnp.maximum(pre, 0.0) + jnp.log(one)
-            sig = jnp.where(pre >= 0, 1.0, t) / one
-            act_s[pl.ds(n, cout, stride=cells), :] = 0.3 * pre + 0.7 * soft
-            up = up_s[pl.ds(n, cout, stride=cells), :]
-            d16 = (up * (0.3 + 0.7 * sig)).astype(BF16)
-            dpad[1 + n // cols, 1 + n % cols] = d16
-            d = d16.astype(F32)
-            sd[0:cout, n * depth:(n + 1) * depth] = ahead(d, lane).astype(BF16)
-            sd[cout:2 * cout, n * depth:(n + 1) * depth] = d16
-            sd[2 * cout:, n * depth:(n + 1) * depth] = behind(d, lane).astype(BF16)
+    step = 2 if cols % 2 == 0 else 1
+    sub = cout // 2 if cout % 32 == 0 else cout
+
+    def columns(lo, hi):
+        for x in range(rows):
+            for y in range(lo, hi):
+                n = x * cols + y
+                for a in range(3):
+                    for b in range(3):
+                        g = a * 3 + b
+                        col[g * cin:(g + 1) * cin, n * depth:(n + 1) * depth] = pad[x + a, y + b]
+
+    def product(m):
+        at = slice(m * depth, (m + step) * depth)
+        ys[:, at] = jnp.dot(wtt[...], col[0:9 * cin, at], preferred_element_type=F32)
+
+    def pointwise(n, h):
+        at = slice(n * depth, (n + 1) * depth)
+        lane = lax.broadcasted_iota(jnp.int32, (sub, depth), 1)
+        y0, y1, y2 = (ys[c * cout + h:c * cout + h + sub, at] for c in range(3))
+        pre = behind(y0, lane) + y1 + ahead(y2, lane) + bias[h:h + sub]
+        t = jnp.exp(-jnp.abs(pre))
+        one = 1.0 + t
+        soft = jnp.maximum(pre, 0.0) + jnp.log(one)
+        sig = jnp.where(pre >= 0, 1.0, t) / one
+        spot = pl.ds(h * cells + n, sub, stride=cells)
+        act_s[spot, :] = 0.3 * pre + 0.7 * soft
+        d16 = (up_s[spot, :] * (0.3 + 0.7 * sig)).astype(BF16)
+        dpad[1 + n // cols, 1 + n % cols, h:h + sub, :] = d16
+        d = d16.astype(F32)
+        sd[h:h + sub, at] = ahead(d, lane).astype(BF16)
+        sd[cout + h:cout + h + sub, at] = d16
+        sd[2 * cout + h:2 * cout + h + sub, at] = behind(d, lane).astype(BF16)
+
+    def forward(lo, hi):
+        columns(lo, hi)
+        ms = [x * cols + y for x in range(rows) for y in range(lo, hi, step)]
+        product(ms[0])
+        for i, m in enumerate(ms):
+            if i + 1 < len(ms):
+                product(ms[i + 1])
+            for n in range(m, m + step):
+                for h in range(0, cout, sub):
+                    pointwise(n, h)
+
+    halo_recv(pad, hs1, hr1, live)
+    forward(0, half)
+    if half < cols:
+        halo_recv(pad, hs1, hr1, late, 1)
+        forward(half, cols)
 
     dw = lax.dot_general(col[...], sd[...], (((1,), (1,)), ((), ())), preferred_element_type=F32)
-    k9, o2, half = 9 * cin, 2 * cout, 5 * cin
-    stage[k9 + half - cin:, :] = jnp.zeros_like(stage[k9 + half - cin:, :])
+    k9, o2, five = 9 * cin, 2 * cout, 5 * cin
+    stage[k9 + five - cin:, :] = jnp.zeros_like(stage[k9 + five - cin:, :])
     stage[0:k9, :] = dw[0:k9, 0:o2]
-    stage[k9:k9 + half, 0:cout] = dw[0:half, o2:]
-    stage[k9:k9 + k9 - half, cout:] = dw[half:k9, o2:]
-    brow = k9 + k9 - half
+    stage[k9:k9 + five, 0:cout] = dw[0:five, o2:]
+    stage[k9:k9 + k9 - five, cout:] = dw[five:k9, o2:]
+    brow = k9 + k9 - five
     stage[brow:brow + 16, cout:] = dw[k9:, cout:o2]
     for q in range(owners):
         part[q] = stage[q * crows:(q + 1) * crows, :].astype(BF16)
@@ -304,7 +334,7 @@
 
     backward(0, cells)
     when(mine, reduce_own, every)
-    halo_recv(hin, hs2, hr2)
+    halo_recv(hin, hs2, hr2, live)
     for x in range(1, rows + 1):
         for y in range(1, cols + 1):
             spots = []
@@ -326,8 +356,9 @@
         when(p < owners, lambda: ag(p, p, p).wait_recv(), every)
 
     each(n_samp, ag_recv)
-    halo_sent(pad, hs1, hr1)
-    halo_sent(hin, hs2, hr2)
+    halo_sent(pad, hs1, hr1, live)
+    halo_sent(pad, hs1, hr1, late, 1)
+    halo_sent(hin, hs2, hr2, live)
     each(n_samp, rs_sent)
 
     def own_sent():
@@ -396,13 +427,13 @@
             v((cout * cells, depth), F32), v((cin * cells, depth), F32),
             v((rows + 2, cols + 2, cin, depth), BF16), v((rows + 2, cols + 2, cout, depth), BF16),
             v((rows + 2, cols + 2, cin, depth), BF16), v((rows + 2, cols + 2, cin, depth), BF16),
-            v((9 * cin + 16, cells * depth), BF16), v((9 * cout, cells * depth), BF16),
+            v((9 * cin + 16, cells * depth), BF16), v((3 * cout, cells * depth), F32), v((9 * cout, cells * depth), BF16),
             v((3 * cout, cells * depth), BF16),
             v((9 * cin, 3 * cout), BF16), v((3 * cout, 9 * cin), BF16), v((3 * cin, 9 * cout), BF16),
             v((9, 3 * cin, cout), BF16),
             v((owners * crows, 2 * cout), F32), v((owners, crows, 2 * cout), BF16),
             v((sizes[0], crows, 2 * cout), BF16), v((group, crows, 2 * cout), BF16),
-            dma((4,)), dma((8,)), dma((8,)), dma((8,)), dma((8,)),
+            dma((4,)), dma((16,)), dma((16,)), dma((8,)), dma((8,)),
             dma((owners,)), dma((sizes[0],)), dma((group,)), dma((group,)),
             dma((sizes[0],)), dma((owners,)),
         ],

time: 25.3 us -> 25.3 us (level)
  no operation moved by 1% of the time
where the time goes in v3:
time: 25.3 us; the launch traced here: 25.2 us
  Pallas kernels  24.5 us (97%)
  between operations  0.64 us (3%)
    pallas_call x1, Pallas kernels, per_device(): pl.pallas_call(functools.partial(kernel, (rows, cols, cin, cout, depth),...  23.6 us
    pallas_call x1, Pallas kernels, per_device(): pl.pallas_call(functools.partial(finish, norm, cin, cout), out_shape=(act...  0.93 us

profile of v3, /device:TPU:0, one launch (start us, length us, event | category | flops | bytes accessed | tf_op | source)
XLA Modules:
  0.0 25.2 jit_solution(9093928203013326229)
XLA Ops:
  0.6 23.6 %shard_map.75 = (bf16[1024,128]{1,0:T(8,128)(2,1)S(1)}, bf16[512,128]{1,0:T(8,128)(2,1)S(1)}, bf16[7,64,128]{2,1,0:T(8,128)(2,1)S(1)}) custom-call(bf16[512,128]{1,0:T(8,128)(2,1)} %bitcast.14, bf16[27,32,64]{2,1,0:T(8,128)(2,1)} %bitcast.13, f32[1,64]{1,0:T(1,128)} %bitcast.15, bf16[1024,128]{1,0:T(8,128)(2,1)} %bitcast.12), custom_call_target="tpu_custom_call" | custom-call | tf_op jit(solution)/shard_map/pallas_call | solution.py:419
  24.2 0.9 %shard_map.76 = (bf16[1024,128]{1,0:T(8,128)(2,1)}, bf16[512,128]{1,0:T(8,128)(2,1)}, f32[27,32,64]{2,1,0:T(8,128)}, f32[1,64]{1,0:T(1,128)}) custom-call(bf16[1024,128]{1,0:T(8,128)(2,1)S(1)} %get-tuple-element.11.act_ref, bf16[512,128]{1,0:T(8,128)(2,1)S(1)} %get-tuple-element.12.ig_ref, bf16[7,64,128]{2,1,0:T(8,128)(2,1)S(1)} %get-tuple-element.13.gat), custom_call_target="tpu_custom_call" | custom-call | tf_op jit(solution)/shard_map/pallas_call | solution.py:451

commit v4 on v3

--- a/solution.py
+++ b/solution.py
@@ -43,7 +43,7 @@
     vol_hbm, w_hbm, bias_hbm, up_hbm,
     act_ref, ig_ref, gat,
     vol_ref, w_ref, bias_ref, up_ref,
-    vol_s, up_s, act_s, ig_s, pad, dpad, hout, hin, col, ys, dcol, sd, wt, wtt, wb, wbs, stage, part, r1, r2,
+    vol_s, up_s, act_s, ig_s, pad, dpad, hout, hin, col, ys, act_c, up_c, dcol, sd, wt, wtt, wb, wbs, stage, part, r1, r2,
     ls, hs1, hr1, hs2, hr2, s1, v1, s2, v2, s3, v3,
 ):
     rows, cols, cin, cout, depth = dims
@@ -160,6 +160,8 @@
             wbs[g, c * cin:(c + 1) * cin, :] = block
     wtt[...] = wt[...].T
     up_s[...] = up_ref[...].astype(F32)
+    for n in range(cells):
+        up_c[n] = up_s[pl.ds(n, cout, stride=cells), :]
     col[9 * cin:, :] = jnp.ones((16, cells * depth), BF16)
     eye = lax.broadcasted_iota(jnp.int32, (cout, cout), 0) == lax.broadcasted_iota(jnp.int32, (cout, cout), 1)
     bias = jnp.sum(jnp.where(eye, bias_ref[...], 0.0), axis=1, keepdims=True)
@@ -196,9 +198,8 @@
         one = 1.0 + t
         soft = jnp.maximum(pre, 0.0) + jnp.log(one)
         sig = jnp.where(pre >= 0, 1.0, t) / one
-        spot = pl.ds(h * cells + n, sub, stride=cells)
-        act_s[spot, :] = 0.3 * pre + 0.7 * soft
-        d16 = (up_s[spot, :] * (0.3 + 0.7 * sig)).astype(BF16)
+        act_c[n, h:h + sub, :] = 0.3 * pre + 0.7 * soft
+        d16 = (up_c[n, h:h + sub, :] * (0.3 + 0.7 * sig)).astype(BF16)
         dpad[1 + n // cols, 1 + n % cols, h:h + sub, :] = d16
         d = d16.astype(F32)
         sd[h:h + sub, at] = ahead(d, lane).astype(BF16)
@@ -276,7 +277,6 @@
 
     for d in live:
         pl.when(has(*DIRS[d]))(lambda: outside(d))
-    act_ref[...] = act_s[...].astype(BF16)
     for x in range(rows):
         for y in range(cols):
             n = x * cols + y
@@ -350,6 +350,9 @@
                 ig_s[at, :] = total
     ig_ref[...] = ig_s[...].astype(BF16)
     when(mine, gather_own, every)
+    for n in range(cells):
+        act_s[pl.ds(n, cout, stride=cells), :] = act_c[n]
+    act_ref[...] = act_s[...].astype(BF16)
 
     def ag_recv(k):
         p = lax.rem(me + k, n_samp)
@@ -427,7 +430,8 @@
             v((cout * cells, depth), F32), v((cin * cells, depth), F32),
             v((rows + 2, cols + 2, cin, depth), BF16), v((rows + 2, cols + 2, cout, depth), BF16),
             v((rows + 2, cols + 2, cin, depth), BF16), v((rows + 2, cols + 2, cin, depth), BF16),
-            v((9 * cin + 16, cells * depth), BF16), v((3 * cout, cells * depth), F32), v((9 * cout, cells * depth), BF16),
+            v((9 * cin + 16, cells * depth), BF16), v((3 * cout, cells * depth), F32),
+            v((cells, cout, depth), F32), v((cells, cout, depth), F32), v((9 * cout, cells * depth), BF16),
             v((3 * cout, cells * depth), BF16),
             v((9 * cin, 3 * cout), BF16), v((3 * cout, 9 * cin), BF16), v((3 * cin, 9 * cout), BF16),
             v((9, 3 * cin, cout), BF16),

time: 25.3 us -> 25.2 us (level)
  no operation moved by 1% of the time
where the time goes in v4:
time: 25.2 us; the launch traced here: 25 us
  Pallas kernels  24.4 us (97%)
  between operations  0.64 us (3%)
    pallas_call x1, Pallas kernels, per_device(): pl.pallas_call(functools.partial(kernel, (rows, cols, cin, cout, depth),...  23.5 us
    pallas_call x1, Pallas kernels, per_device(): pl.pallas_call(functools.partial(finish, norm, cin, cout), out_shape=(act...  0.93 us

profile of v4, /device:TPU:0, one launch (start us, length us, event | category | flops | bytes accessed | tf_op | source)
XLA Modules:
  0.0 25.0 jit_solution(5334681591737372135)
XLA Ops:
  0.6 23.5 %shard_map.75 = (bf16[1024,128]{1,0:T(8,128)(2,1)S(1)}, bf16[512,128]{1,0:T(8,128)(2,1)S(1)}, bf16[7,64,128]{2,1,0:T(8,128)(2,1)S(1)}) custom-call(bf16[512,128]{1,0:T(8,128)(2,1)} %bitcast.14, bf16[27,32,64]{2,1,0:T(8,128)(2,1)} %bitcast.13, f32[1,64]{1,0:T(1,128)} %bitcast.15, bf16[1024,128]{1,0:T(8,128)(2,1)} %bitcast.12), custom_call_target="tpu_custom_call" | custom-call | tf_op jit(solution)/shard_map/pallas_call | solution.py:422
  24.1 0.9 %shard_map.76 = (bf16[1024,128]{1,0:T(8,128)(2,1)}, bf16[512,128]{1,0:T(8,128)(2,1)}, f32[27,32,64]{2,1,0:T(8,128)}, f32[1,64]{1,0:T(1,128)}) custom-call(bf16[1024,128]{1,0:T(8,128)(2,1)S(1)} %get-tuple-element.11.act_ref, bf16[512,128]{1,0:T(8,128)(2,1)S(1)} %get-tuple-element.12.ig_ref, bf16[7,64,128]{2,1,0:T(8,128)(2,1)S(1)} %get-tuple-element.13.gat), custom_call_target="tpu_custom_call" | custom-call | tf_op jit(solution)/shard_map/pallas_call | solution.py:455

commit v5 on v4

--- a/solution.py
+++ b/solution.py
@@ -273,7 +273,6 @@
             for n, (x, y) in enumerate(pair):
                 u0, u1, u2 = (out[c * cin:(c + 1) * cin, n * depth:(n + 1) * depth] for c in range(3))
                 hout[x, y] = (ahead(u0, lane_i) + u1 + behind(u2, lane_i)).astype(BF16)
-        halo(hin, hs2, hr2, d).start()
 
     for d in live:
         pl.when(has(*DIRS[d]))(lambda: outside(d))
@@ -334,6 +333,12 @@
 
     backward(0, cells)
     when(mine, reduce_own, every)
+    for d in live:
+        pl.when(has(*DIRS[d]))(lambda: halo(hin, hs2, hr2, d).start())
+    when(mine, gather_own, every)
+    for n in range(cells):
+        act_s[pl.ds(n, cout, stride=cells), :] = act_c[n]
+    act_ref[...] = act_s[...].astype(BF16)
     halo_recv(hin, hs2, hr2, live)
     for x in range(1, rows + 1):
         for y in range(1, cols + 1):
@@ -349,10 +354,6 @@
                     total = total + hin[spot].astype(F32)
                 ig_s[at, :] = total
     ig_ref[...] = ig_s[...].astype(BF16)
-    when(mine, gather_own, every)
-    for n in range(cells):
-        act_s[pl.ds(n, cout, stride=cells), :] = act_c[n]
-    act_ref[...] = act_s[...].astype(BF16)
 
     def ag_recv(k):
         p = lax.rem(me + k, n_samp)

time: 25.2 us -> 25.2 us (level)
  no operation moved by 1% of the time
where the time goes in v5:
time: 25.2 us; the launch traced here: 25 us
  Pallas kernels  24.4 us (97%)
  between operations  0.64 us (3%)
    pallas_call x1, Pallas kernels, per_device(): pl.pallas_call(functools.partial(kernel, (rows, cols, cin, cout, depth),...  23.5 us
    pallas_call x1, Pallas kernels, per_device(): pl.pallas_call(functools.partial(finish, norm, cin, cout), out_shape=(act...  0.93 us

profile of v5, /device:TPU:0, one launch (start us, length us, event | category | flops | bytes accessed | tf_op | source)
XLA Modules:
  0.0 25.0 jit_solution(7476408954649662283)
XLA Ops:
  0.6 23.5 %shard_map.75 = (bf16[1024,128]{1,0:T(8,128)(2,1)S(1)}, bf16[512,128]{1,0:T(8,128)(2,1)S(1)}, bf16[7,64,128]{2,1,0:T(8,128)(2,1)S(1)}) custom-call(bf16[512,128]{1,0:T(8,128)(2,1)} %bitcast.14, bf16[27,32,64]{2,1,0:T(8,128)(2,1)} %bitcast.13, f32[1,64]{1,0:T(1,128)} %bitcast.15, bf16[1024,128]{1,0:T(8,128)(2,1)} %bitcast.12), custom_call_target="tpu_custom_call" | custom-call | tf_op jit(solution)/shard_map/pallas_call | solution.py:423
  24.1 0.9 %shard_map.76 = (bf16[1024,128]{1,0:T(8,128)(2,1)}, bf16[512,128]{1,0:T(8,128)(2,1)}, f32[27,32,64]{2,1,0:T(8,128)}, f32[1,64]{1,0:T(1,128)}) custom-call(bf16[1024,128]{1,0:T(8,128)(2,1)S(1)} %get-tuple-element.11.act_ref, bf16[512,128]{1,0:T(8,128)(2,1)S(1)} %get-tuple-element.12.ig_ref, bf16[7,64,128]{2,1,0:T(8,128)(2,1)S(1)} %get-tuple-element.13.gat), custom_call_target="tpu_custom_call" | custom-call | tf_op jit(solution)/shard_map/pallas_call | solution.py:456
